TPU v7x, 32 devices: a whole 2x2x4 slice. The times are simulated.
32 devices in a mesh: group: 4 (over y, x), tile: 4 (over z), video: 2 (over core).
Axes of the slice: x: 2, y: 2, z: 4, core: 2. Of those that a mesh axis runs over, the one named last changes fastest.
Arguments:
- features: bfloat16 [8, 8, 16, 24, 384], P(('video', 'tile'), 'group'), parts along dimension 0, may hold values from -6 to 6
- group_slot: int32 [4], replicated, may hold values from 0 to 3, each once
- margins: int32 [4, 4], P('tile'), may hold values from 0 to 4, as said below
- norm_gain: float32 [384], replicated, may hold values from 0.1 to 1.9
- kernel: bfloat16 [3, 3, 3, 384, 384], replicated, may hold values from -0.0625 to 0.0625
- conv_bias: float32 [384], replicated, may hold values from -3 to 3
Outputs:
- decoded: bfloat16 [8, 8, 16, 24, 384], P(('video', 'tile'), 'group'), parts along dimension 0
There are 2 independent parts, one for each index of `video`. A program takes and returns all parts, laid end to end along the dimension named above; an argument that names none is the same for every part. Nothing has to cross between parts.
Inputs may be any that keep to these rules, and one draw needn't show every extreme that they name: group_slot is a permutation of 0 to 3. margins[t] is (left, right, up, down) of tile t; a margin is 0 exactly at the image's border and 1 to 4 elsewhere; the margin a tile has toward a neighbour equals the neighbour's margin back; left and right margins depend only on the tile's column, up and down margins are the same for all columns; some margin equals 4.
All inputs are finite; a program needn't handle non-finite values.
Results may differ from a plain program's by a relative error of at most 0.0043.
Values may be sent and summed in bfloat16 or wider, within the bound.
A program may use at most 128 MiB of HBM per device.

v0:
```python
import jax
import jax.numpy as jnp
from jax import lax
from jax.sharding import PartitionSpec as P

M = 4
GRID_R = 2


def passed_along(shard, axis, by):
    peers = lax.axis_size(axis)
    pairs = [(i, i + by) for i in range(peers) if 0 <= i + by < peers]
    return lax.ppermute(shard, axis, pairs)


def activate(values, norm_gain):
    widened = values.astype(jnp.float32)
    inv_norm = lax.rsqrt(jnp.mean(widened * widened, axis=-1, keepdims=True) + 1e-06)
    return jax.nn.silu(widened * inv_norm * norm_gain).astype(jnp.bfloat16)


def convolve(padded, kernel, conv_bias, row_count, col_count):
    frame_count = padded.shape[0] - 2
    channels = padded.shape[-1]
    summed = jnp.zeros((frame_count * row_count * col_count, kernel.shape[-1]), jnp.float32)
    for tap_time in range(3):
        for tap_row in range(3):
            window = padded[tap_time : tap_time + frame_count, tap_row : tap_row + row_count]
            stacked = jnp.concatenate(
                [window[:, :, tap_col : tap_col + col_count] for tap_col in range(3)], axis=-1
            )
            flattened = stacked.reshape(frame_count * row_count * col_count, 3 * channels)
            summed = summed + jnp.dot(
                flattened,
                kernel[tap_time, tap_row].reshape(3 * channels, -1),
                preferred_element_type=jnp.float32,
            )
    return summed.reshape(frame_count, row_count, col_count, -1) + conv_bias


def window_band(core, near, far):
    position = jnp.arange(core + 2 * M, dtype=jnp.int32)
    return (position >= M - near) & (position < M + core + far)


def rim_weight(step, core, near, far):
    position = jnp.arange(core, dtype=jnp.int32)
    if step == 1:
        distance = position + 1
        margin = near
    elif step == -1:
        distance = core - position
        margin = far
    else:
        return jnp.ones((core,), jnp.float32)
    margin_f = margin.astype(jnp.float32)
    return jnp.maximum(margin_f + 1.0 - distance.astype(jnp.float32), 0.0) / (margin_f + 1.0)


def rim_source(step, core):
    if step == 1:
        return (core - M, M, 0)
    if step == -1:
        return (0, M, M + core)
    return (0, core, M)


def panel_source(step, core):
    if step == 1:
        return (M + core, M, 0)
    if step == -1:
        return (0, M, core - M)
    return (M, core, 0)


def blend_add(weighted, weight_sum, panel, step_r, step_c, row_dest, col_dest, reaches):
    core_h = weighted.shape[1]
    core_w = weighted.shape[2]
    row_len = panel.shape[1]
    col_len = panel.shape[2]
    placed = jnp.pad(
        panel.astype(jnp.float32),
        (
            (0, 0),
            (row_dest, core_h - row_dest - row_len),
            (col_dest, core_w - col_dest - col_len),
            (0, 0),
        ),
    )
    weight = (
        rim_weight(step_r, core_h, reaches[2], reaches[3])[:, None]
        * rim_weight(step_c, core_w, reaches[0], reaches[1])[None, :]
    )
    return (weighted + placed * weight[None, :, :, None], weight_sum + weight)


def gather_rims(source_block, grid_cols):
    core_h = source_block.shape[1]
    core_w = source_block.shape[2]
    result = jnp.pad(source_block, ((0, 0), (M, M), (M, M), (0, 0)))
    for step_r in (1, 0, -1):
        for step_c in (1, 0, -1):
            if step_r == 0 and step_c == 0:
                continue
            row_first, row_len, row_dest = rim_source(step_r, core_h)
            col_first, col_len, col_dest = rim_source(step_c, core_w)
            outgoing = source_block[
                :, row_first : row_first + row_len, col_first : col_first + col_len
            ]
            incoming = passed_along(outgoing, "tile", step_r * grid_cols + step_c)
            result = result.at[:, row_dest : row_dest + row_len, col_dest : col_dest + col_len].set(
                incoming
            )
    return result


def local(features, group_slot, margins, norm_gain, kernel, conv_bias):
    own_block = features[0]
    frame_count, core_h, core_w, channels = own_block.shape
    grid_cols = lax.axis_size("tile") // GRID_R
    reaches = margins[0]
    wanted = group_slot[lax.axis_index("group")] - 1
    chosen = jnp.zeros((2, core_h, core_w, channels), jnp.bfloat16)
    pieces = lax.all_gather(own_block[None], "group", axis=0, tiled=True)
    first_dev = jnp.int32(0)
    for offset in range(pieces.shape[0]):
        matches = group_slot[first_dev + offset] == wanted
        chosen = chosen + jnp.where(matches, pieces[offset], jnp.zeros_like(pieces[offset]))
    buffered = gather_rims(jnp.concatenate([chosen, own_block], axis=0), grid_cols)
    activated = activate(buffered, norm_gain)
    padded = jnp.pad(activated, ((0, 0), (1, 1), (1, 1), (0, 0)))
    weighted = jnp.zeros((frame_count, core_h, core_w, channels), jnp.float32)
    weight_sum = jnp.zeros((core_h, core_w), jnp.float32)
    inside = (
        window_band(core_h, reaches[2], reaches[3])[:, None]
        & window_band(core_w, reaches[0], reaches[1])[None, :]
    )
    inside = jnp.pad(inside, 1)
    masked = jnp.where(inside[None, :, :, None], padded, jnp.zeros_like(padded))
    outputs = convolve(masked, kernel, conv_bias, core_h + 2 * M, core_w + 2 * M).astype(
        jnp.bfloat16
    )
    for step_r in (1, 0, -1):
        for step_c in (1, 0, -1):
            row_first, row_len, row_dest = panel_source(step_r, core_h)
            col_first, col_len, col_dest = panel_source(step_c, core_w)
            outgoing = outputs[:, row_first : row_first + row_len, col_first : col_first + col_len]
            if step_r == 0 and step_c == 0:
                incoming = outgoing
            else:
                incoming = passed_along(outgoing, "tile", step_r * grid_cols + step_c)
            weighted, weight_sum = blend_add(
                weighted, weight_sum, incoming, step_r, step_c, row_dest, col_dest, reaches
            )
    return (weighted / weight_sum[None, :, :, None]).astype(jnp.bfloat16)[None]


def solution(mesh):
    return jax.shard_map(
        local,
        mesh=mesh,
        in_specs=(
            P(("video", "tile"), "group", None, None, None),
            P(),
            P("tile", None),
            P(),
            P(),
            P(),
        ),
        out_specs=P(("video", "tile"), "group", None, None, None),
        check_vma=False,
    )
```

profile of v0, /device:TPU:0, one launch (start us, length us, event | category | flops | bytes accessed | tf_op | source)
XLA Modules:
  0.0 182.1 jit_solution(15480783370561871145)
XLA Ops:
  23.2 5.7 %fusion.21 = (bf16[1,1,3,384,384]{4,3,2,1,0:T(8,128)(2,1)}, bf16[1,1,3,384,384]{4,3,2,1,0:T(8,128)(2,1)}, bf16[1,1,3,384,384]{4,3,2,1,0:T(8,128)(2,1)}, bf16[1,1...) fusion(bf16[3,3,3,384,384]{4,3,2,1,0:T(8,128)(2,1)} %param.26), kind=kLoop, calls=%fused_computation.92 | loop fusion | bytes 15925248 | tf_op jit(solution)/shard_map/slice | solution.py:35
  28.9 20.4 %all-gather.2.cloned.1.call-done = bf16[4,2,16,24,384]{4,3,2,1,0:T(8,128)(2,1)} async-done(((bf16[1,2,16,24,384]{4,3,2,1,0:T(8,128)(2,1)}), bf16[4,2,16,24,384]{4,3,2,1,0:T(8,128)(2,1)}) %all-gather.2.cloned.1.call-update) | async-done | bytes 2359312 | tf_op jit(solution)/shard_map/all_gather | solution.py:124
  51.3 4.3 %collective-permute-start.1 = (bf16[4,4,24,384]{3,2,1,0:T(8,128)(2,1)S(1)}, bf16[4,4,24,384]{3,2,1,0:T(8,128)(2,1)S(1)}, u32[]{:S(2)}, u32[]{:S(2)}) collective-permute-start(bf16[4,4,24,384]{3,2,1,0:T(8,128)(2,1)S(1)} %get-tuple-element.150), channel_id=1, source_target_pairs={{0,4},{2,6},{1,5},{3,7},{8,12},{10,14},{9,13},{11,15},{16,20},{18,... | collective-permute-start | bytes 884744 | tf_op jit(solution)/shard_map/ppermute | solution.py:13
  56.4 2.2 %collective-permute-start = (bf16[4,4,4,384]{3,2,1,0:T(4,128)(2,1)S(1)}, bf16[4,4,4,384]{3,2,1,0:T(4,128)(2,1)S(1)}, u32[]{:S(2)}, u32[]{:S(2)}) collective-permute-start(bf16[4,4,4,384]{3,2,1,0:T(4,128)(2,1)S(1)} %get-tuple-element.146), channel_id=1, source_target_pairs={{0,6},{1,7},{8,14},{9,15},{16,22},{17,23},{24,30},{25,31}} | collective-permute-start | bytes 147464 | tf_op jit(solution)/shard_map/ppermute | solution.py:13
  60.1 2.4 %collective-permute-start.2 = (bf16[4,4,4,384]{3,2,1,0:T(4,128)(2,1)}, bf16[4,4,4,384]{3,2,1,0:T(4,128)(2,1)}, u32[]{:S(2)}, u32[]{:S(2)}) collective-permute-start(bf16[4,4,4,384]{3,2,1,0:T(4,128)(2,1)} %get-tuple-element.147), channel_id=1, source_target_pairs={{0,2},{2,4},{4,6},{1,3},{3,5},{5,7},{8,10},{10,12},{12,14},{9,11},... | collective-permute-start | bytes 147464 | tf_op jit(solution)/shard_map/ppermute | solution.py:13
  66.0 7.2 %collective-permute-start.3 = (bf16[4,16,4,384]{3,2,1,0:T(4,128)(2,1)S(1)}, bf16[4,16,4,384]{3,2,1,0:T(4,128)(2,1)}, u32[]{:S(2)}, u32[]{:S(2)}) collective-permute-start(bf16[4,16,4,384]{3,2,1,0:T(4,128)(2,1)S(1)} %get-tuple-element.152), channel_id=1, source_target_pairs={{0,2},{2,4},{4,6},{1,3},{3,5},{5,7},{8,10},{10,12},{12,14},{9,11},... | collective-permute-start | bytes 589832 | tf_op jit(solution)/shard_map/ppermute | solution.py:13
  75.1 2.3 %scatter.29 = bf16[4,24,32,384]{3,2,1,0:T(8,128)(2,1)S(1)} dynamic-update-slice(bf16[4,24,32,384]{3,2,1,0:T(8,128)(2,1)S(1)} %constant_dynamic-update-slice_fusion.4, bf16[4,4,24,384]{3,2,1,0:T(8,128)(2,1)S(1)} %dynamic-slice_select_fusion, s32[]{:T(128)} %constant.276.clone.1, s32[]{:T(128)} %bitcast.10, s32[]{:T(128)} %bitcast.11, s32[]{:T(128)} %constant.276.clone.1) | dynamic-update-slice | bytes 589828 | tf_op jit(solution)/shard_map/scatter | solution.py:111
  79.0 3.4 %dynamic-slice_select_fusion.1 = bf16[4,4,4,384]{3,2,1,0:T(4,128)(2,1)} fusion(bf16[4,4,4,384]{3,2,1,0:T(4,128)(2,1)} %collective-permute-done.2, bf16[4,24,32,384]{3,2,1,0:T(8,128)(2,1)S(1)} %scatter.29, s32[]{:T(128)} %bitcast.12, s32[]{:T(128)} %bitcast.13, pred[]{:T(512)} %and_reduce_fusion), kind=kLoop, calls=%fused_computation.66 | loop fusion | flops 24576 | bytes 147465 | tf_op jit(solution)/shard_map/select.10
  82.3 2.2 %scatter.30 = bf16[4,24,32,384]{3,2,1,0:T(8,128)(2,1)S(1)} dynamic-update-slice(bf16[4,24,32,384]{3,2,1,0:T(8,128)(2,1)S(1)} %scatter.29, bf16[4,4,4,384]{3,2,1,0:T(4,128)(2,1)} %dynamic-slice_select_fusion.1, s32[]{:T(128)} %constant.276.clone.1, s32[]{:T(128)} %bitcast.12, s32[]{:T(128)} %bitcast.13, s32[]{:T(128)} %constant.276.clone.1) | dynamic-update-slice | bytes 98308 | tf_op jit(solution)/shard_map/scatter | solution.py:111
  86.6 8.5 %collective-permute-done.6 = bf16[4,4,24,384]{3,2,1,0:T(8,128)(2,1)S(1)} collective-permute-done((bf16[4,4,24,384]{3,2,1,0:T(8,128)(2,1)S(1)}, bf16[4,4,24,384]{3,2,1,0:T(8,128)(2,1)S(1)}, u32[]{:S(2)}, u32[]{:S(2)}) %collective-permute-start.6) | collective-permute-done | bytes 294944 | tf_op jit(solution)/shard_map/ppermute | solution.py:13
  97.7 2.2 %fusion.7 = bf16[4,24,32,384]{3,2,1,0:T(8,128)(2,1)S(1)} fusion(bf16[4,24,32,384]{3,2,1,0:T(8,128)(2,1)S(1)} %constant_dynamic-update-slice_fusion, f32[384]{0:T(512)} %param.25, f32[4,24,32]{2,1,0:T(8,128)S(1)} %add_rsqrt_fusion), kind=kLoop, calls=%fused_computation.9 | loop fusion | flops 9437184 | bytes 4732416 | tf_op jit(solution)/shard_map/convert_element_type | solution.py:19
  101.5 4.5 %fusion.23 = (bf16[2,24,32,384]{3,2,1,0:T(8,128)(2,1)S(1)}, bf16[2,24,32,384]{3,2,1,0:T(8,128)(2,1)S(1)}, bf16[2,24,32,384]{3,2,1,0:T(8,128)(2,1)}, bf16[2,24,32...) fusion(bf16[4,26,34,384]{3,2,1,0:T(8,128)(2,1)S(1)} %pad_select, ...), kind=kLoop, calls=%fused_computation.94 | loop fusion | bytes 18874368 | tf_op jit(solution)/shard_map/slice | solution.py:30
  105.9 6.3 %fusion.22 = (bf16[2,24,32,384]{3,2,1,0:T(8,128)(2,1)}, bf16[2,24,32,384]{3,2,1,0:T(8,128)(2,1)}, bf16[2,24,32,384]{3,2,1,0:T(8,128)(2,1)}, bf16[2,24,32,384]{3,...) fusion(bf16[4,26,34,384]{3,2,1,0:T(8,128)(2,1)S(1)} %pad_select, ...), kind=kLoop, calls=%fused_computation.93 | loop fusion | bytes 44826624 | tf_op jit(solution)/shard_map/slice | solution.py:30
  112.2 3.4 %pad_maximum_fusion = (bf16[2,24,32,1152]{3,2,1,0:T(8,128)(2,1)S(1)}, bf16[2,24,32,1152]{3,2,1,0:T(8,128)(2,1)S(1)}) fusion(bf16[2,24,32,384]{3,2,1,0:T(8,128)(2,1)} %get-tuple-element.134, bf16[2,24,32,384]{3,2,1,0:T(8,128)(2,1)} %get-tuple-element.135, bf16[2,24,32,384]{3,2,1,0:T(8,128)(2,1)} %get-tuple-element.136, ...), kind=kLoop, calls=%fused_computation.10 | loop fusion | flops 21233664 | bytes 14155776 | tf_op jit(solution)/shard_map/concatenate | solution.py:29
  117.8 3.6 %convolution_add_fusion.7 = f32[1536,384]{1,0:T(8,128)} fusion(f32[1536,384]{1,0:T(8,128)S(1)} %fusion.31, bf16[1536,1152]{1,0:T(8,128)(2,1)S(1)} %bitcast.65, bf16[1152,384]{1,0:T(8,128)(2,1)S(1)} %bitcast.79), kind=kOutput, calls=%fused_computation.27 | convolution fusion | flops 1359544320 | bytes 9142272 | tf_op jit(solution)/shard_map/dot_general | solution.py:33
  124.6 3.9 %convolution_add_fusion.6 = f32[1536,384]{1,0:T(8,128)S(1)} fusion(f32[1536,384]{1,0:T(8,128)} %convolution_add_fusion.7, bf16[1536,1152]{1,0:T(8,128)(2,1)S(1)} %bitcast.66, bf16[1152,384]{1,0:T(8,128)(2,1)S(1)} %bitcast.78), kind=kOutput, calls=%fused_computation.26 | convolution fusion | flops 1359544320 | bytes 9142272 | tf_op jit(solution)/shard_map/dot_general | solution.py:33
  128.5 2.2 %convolution_add_fusion.5 = f32[1536,384]{1,0:T(8,128)S(1)} fusion(f32[1536,384]{1,0:T(8,128)S(1)} %convolution_add_fusion.6, bf16[1536,1152]{1,0:T(8,128)(2,1)S(1)} %bitcast.62, bf16[1152,384]{1,0:T(8,128)(2,1)S(1)} %bitcast.77), kind=kOutput, calls=%fused_computation.25 | convolution fusion | flops 1359544320 | bytes 9142272 | tf_op jit(solution)/shard_map/dot_general | solution.py:33
  131.9 2.2 %convolution_add_fusion.4 = f32[1536,384]{1,0:T(8,128)S(1)} fusion(f32[1536,384]{1,0:T(8,128)S(1)} %convolution_add_fusion.5, bf16[1536,1152]{1,0:T(8,128)(2,1)S(1)} %bitcast.67, bf16[1152,384]{1,0:T(8,128)(2,1)S(1)} %bitcast.76), kind=kOutput, calls=%fused_computation.24 | convolution fusion | flops 1359544320 | bytes 9142272 | tf_op jit(solution)/shard_map/dot_general | solution.py:33
  134.0 2.1 %convolution_add_fusion.3 = f32[1536,384]{1,0:T(8,128)S(1)} fusion(f32[1536,384]{1,0:T(8,128)S(1)} %convolution_add_fusion.4, bf16[1536,1152]{1,0:T(8,128)(2,1)S(1)} %bitcast.63, bf16[1152,384]{1,0:T(8,128)(2,1)S(1)} %bitcast.75), kind=kOutput, calls=%fused_computation.23 | convolution fusion | flops 1359544320 | bytes 9142272 | tf_op jit(solution)/shard_map/dot_general | solution.py:33
  137.4 2.2 %convolution_add_fusion.2 = f32[1536,384]{1,0:T(8,128)S(1)} fusion(f32[1536,384]{1,0:T(8,128)S(1)} %convolution_add_fusion.3, bf16[1536,1152]{1,0:T(8,128)(2,1)S(1)} %bitcast.68, bf16[1152,384]{1,0:T(8,128)(2,1)S(1)} %bitcast.74), kind=kOutput, calls=%fused_computation.22 | convolution fusion | flops 1359544320 | bytes 9142272 | tf_op jit(solution)/shard_map/dot_general | solution.py:33
  139.6 2.1 %convolution_add_fusion.1 = f32[1536,384]{1,0:T(8,128)S(1)} fusion(f32[1536,384]{1,0:T(8,128)S(1)} %convolution_add_fusion.2, bf16[1536,1152]{1,0:T(8,128)(2,1)S(1)} %bitcast.64, bf16[1152,384]{1,0:T(8,128)(2,1)S(1)} %bitcast.73), kind=kOutput, calls=%fused_computation.21 | convolution fusion | flops 1359544320 | bytes 9142272 | tf_op jit(solution)/shard_map/dot_general | solution.py:33
  148.4 4.5 %collective-permute-start.10 = (bf16[2,4,4,384]{3,2,1,0:T(4,128)(2,1)S(1)}, bf16[2,4,4,384]{3,2,1,0:T(4,128)(2,1)S(1)}, u32[]{:S(2)}, u32[]{:S(2)}) collective-permute-start(bf16[2,4,4,384]{3,2,1,0:T(4,128)(2,1)S(1)} %get-tuple-element.140), channel_id=1, source_target_pairs={{0,2},{2,4},{4,6},{1,3},{3,5},{5,7},{8,10},{10,12},{12,14},{9,11},... | collective-permute-start | bytes 73736 | tf_op jit(solution)/shard_map/ppermute | solution.py:13
  156.2 6.9 %collective-permute-start.9 = (bf16[2,4,24,384]{3,2,1,0:T(8,128)(2,1)S(1)}, bf16[2,4,24,384]{3,2,1,0:T(8,128)(2,1)S(1)}, u32[]{:S(2)}, u32[]{:S(2)}) collective-permute-start(bf16[2,4,24,384]{3,2,1,0:T(8,128)(2,1)S(1)} %get-tuple-element.141), channel_id=1, source_target_pairs={{0,4},{2,6},{1,5},{3,7},{8,12},{10,14},{9,13},{11,15},{16,20},{18,... | collective-permute-start | bytes 442376 | tf_op jit(solution)/shard_map/ppermute | solution.py:13
  165.7 7.4 %collective-permute-done.14 = bf16[2,4,24,384]{3,2,1,0:T(8,128)(2,1)S(1)} collective-permute-done((bf16[2,4,24,384]{3,2,1,0:T(8,128)(2,1)S(1)}, bf16[2,4,24,384]{3,2,1,0:T(8,128)(2,1)S(1)}, u32[]{:S(2)}, u32[]{:S(2)}) %collective-permute-start.14) | collective-permute-done | bytes 147488 | tf_op jit(solution)/shard_map/ppermute | solution.py:13
  (102 shorter events, 47.6 us)
Async XLA Ops:
  6.5 42.7 %all-gather.2.cloned.1.call-start = ((), (), s32[]{:S(2)}) async-start(), calls=%async_computation | async-start | bytes 2949120 | tf_op jit(solution)/shard_map/all_gather | solution.py:124
  28.8 22.2 %copy-start = (bf16[1,2,16,24,384]{4,3,2,1,0:T(8,128)(2,1)S(1)}, bf16[1,2,16,24,384]{4,3,2,1,0:T(8,128)(2,1)}, u32[]{:S(2)}) copy-start(bf16[1,2,16,24,384]{4,3,2,1,0:T(8,128)(2,1)} %param.22) | copy-start | bytes 1769476
  51.3 14.7 %collective-permute-start.1 = (bf16[4,4,24,384]{3,2,1,0:T(8,128)(2,1)S(1)}, bf16[4,4,24,384]{3,2,1,0:T(8,128)(2,1)S(1)}, u32[]{:S(2)}, u32[]{:S(2)}) collective-permute-start(bf16[4,4,24,384]{3,2,1,0:T(8,128)(2,1)S(1)} %get-tuple-element.150), channel_id=1, source_target_pairs={{0,4},{2,6},{1,5},{3,7},{8,12},{10,14},{9,13},{11,15},{16,20},{18,... | collective-permute-start | bytes 884744 | tf_op jit(solution)/shard_map/ppermute | solution.py:13
  56.4 8.3 %collective-permute-start = (bf16[4,4,4,384]{3,2,1,0:T(4,128)(2,1)S(1)}, bf16[4,4,4,384]{3,2,1,0:T(4,128)(2,1)S(1)}, u32[]{:S(2)}, u32[]{:S(2)}) collective-permute-start(bf16[4,4,4,384]{3,2,1,0:T(4,128)(2,1)S(1)} %get-tuple-element.146), channel_id=1, source_target_pairs={{0,6},{1,7},{8,14},{9,15},{16,22},{17,23},{24,30},{25,31}} | collective-permute-start | bytes 147464 | tf_op jit(solution)/shard_map/ppermute | solution.py:13
  58.8 37.5 %collective-permute-start.7 = (bf16[4,4,4,384]{3,2,1,0:T(4,128)(2,1)}, bf16[4,4,4,384]{3,2,1,0:T(4,128)(2,1)}, u32[]{:S(2)}, u32[]{:S(2)}) collective-permute-start(bf16[4,4,4,384]{3,2,1,0:T(4,128)(2,1)} %get-tuple-element.145), channel_id=1, source_target_pairs={{6,0},{7,1},{14,8},{15,9},{22,16},{23,17},{30,24},{31,25}} | collective-permute-start | bytes 147464 | tf_op jit(solution)/shard_map/ppermute | solution.py:13
  60.1 17.4 %collective-permute-start.2 = (bf16[4,4,4,384]{3,2,1,0:T(4,128)(2,1)}, bf16[4,4,4,384]{3,2,1,0:T(4,128)(2,1)}, u32[]{:S(2)}, u32[]{:S(2)}) collective-permute-start(bf16[4,4,4,384]{3,2,1,0:T(4,128)(2,1)} %get-tuple-element.147), channel_id=1, source_target_pairs={{0,2},{2,4},{4,6},{1,3},{3,5},{5,7},{8,10},{10,12},{12,14},{9,11},... | collective-permute-start | bytes 147464 | tf_op jit(solution)/shard_map/ppermute | solution.py:13
  62.5 23.3 %collective-permute-start.5 = (bf16[4,4,4,384]{3,2,1,0:T(4,128)(2,1)}, bf16[4,4,4,384]{3,2,1,0:T(4,128)(2,1)}, u32[]{:S(2)}, u32[]{:S(2)}) collective-permute-start(bf16[4,4,4,384]{3,2,1,0:T(4,128)(2,1)} %get-tuple-element.148), channel_id=1, source_target_pairs={{2,0},{4,2},{6,4},{3,1},{5,3},{7,5},{10,8},{12,10},{14,12},{11,9},... | collective-permute-start | bytes 147464 | tf_op jit(solution)/shard_map/ppermute | solution.py:13
  64.6 21.0 %collective-permute-start.4 = (bf16[4,16,4,384]{3,2,1,0:T(4,128)(2,1)S(1)}, bf16[4,16,4,384]{3,2,1,0:T(4,128)(2,1)S(1)}, u32[]{:S(2)}, u32[]{:S(2)}) collective-permute-start(bf16[4,16,4,384]{3,2,1,0:T(4,128)(2,1)S(1)} %get-tuple-element.151), channel_id=1, source_target_pairs={{2,0},{4,2},{6,4},{3,1},{5,3},{7,5},{10,8},{12,10},{14,12},{11,9},... | collective-permute-start | bytes 589832 | tf_op jit(solution)/shard_map/ppermute | solution.py:13
  66.0 18.6 %collective-permute-start.3 = (bf16[4,16,4,384]{3,2,1,0:T(4,128)(2,1)S(1)}, bf16[4,16,4,384]{3,2,1,0:T(4,128)(2,1)}, u32[]{:S(2)}, u32[]{:S(2)}) collective-permute-start(bf16[4,16,4,384]{3,2,1,0:T(4,128)(2,1)S(1)} %get-tuple-element.152), channel_id=1, source_target_pairs={{0,2},{2,4},{4,6},{1,3},{3,5},{5,7},{8,10},{10,12},{12,14},{9,11},... | collective-permute-start | bytes 589832 | tf_op jit(solution)/shard_map/ppermute | solution.py:13
  77.5 17.6 %collective-permute-start.6 = (bf16[4,4,24,384]{3,2,1,0:T(8,128)(2,1)S(1)}, bf16[4,4,24,384]{3,2,1,0:T(8,128)(2,1)S(1)}, u32[]{:S(2)}, u32[]{:S(2)}) collective-permute-start(bf16[4,4,24,384]{3,2,1,0:T(8,128)(2,1)S(1)} %get-tuple-element.149), channel_id=1, source_target_pairs={{4,0},{6,2},{5,1},{7,3},{12,8},{14,10},{13,9},{15,11},{20,16},{22,... | collective-permute-start | bytes 884744 | tf_op jit(solution)/shard_map/ppermute | solution.py:13
  112.2 3.4 %copy-start.14 = (bf16[1,1,3,384,384]{4,3,2,1,0:T(8,128)(2,1)S(1)}, bf16[1,1,3,384,384]{4,3,2,1,0:T(8,128)(2,1)}, u32[]{:S(2)}) copy-start(bf16[1,1,3,384,384]{4,3,2,1,0:T(8,128)(2,1)} %get-tuple-element.108) | copy-start | bytes 2654212
  117.8 3.7 %copy-start.2 = (bf16[2,24,32,384]{3,2,1,0:T(8,128)(2,1)S(1)}, bf16[2,24,32,384]{3,2,1,0:T(8,128)(2,1)}, u32[]{:S(2)}) copy-start(bf16[2,24,32,384]{3,2,1,0:T(8,128)(2,1)} %get-tuple-element.110) | copy-start | bytes 3538948
  117.8 3.7 %copy-start.3 = (bf16[2,24,32,384]{3,2,1,0:T(8,128)(2,1)S(1)}, bf16[2,24,32,384]{3,2,1,0:T(8,128)(2,1)}, u32[]{:S(2)}) copy-start(bf16[2,24,32,384]{3,2,1,0:T(8,128)(2,1)} %get-tuple-element.111) | copy-start | bytes 3538948
  117.8 3.7 %copy-start.4 = (bf16[2,24,32,384]{3,2,1,0:T(8,128)(2,1)S(1)}, bf16[2,24,32,384]{3,2,1,0:T(8,128)(2,1)}, u32[]{:S(2)}) copy-start(bf16[2,24,32,384]{3,2,1,0:T(8,128)(2,1)} %get-tuple-element.112) | copy-start | bytes 3538948
  124.6 4.0 %copy-start.11 = (bf16[1,1,3,384,384]{4,3,2,1,0:T(8,128)(2,1)S(1)}, bf16[1,1,3,384,384]{4,3,2,1,0:T(8,128)(2,1)}, u32[]{:S(2)}) copy-start(bf16[1,1,3,384,384]{4,3,2,1,0:T(8,128)(2,1)} %get-tuple-element.105) | copy-start | bytes 2654212
  143.9 20.5 %copy-start.15 = (f32[24]{0:T(128)S(1)}, f32[24]{0:T(128)}, u32[]{:S(2)}) copy-start(f32[24]{0:T(128)} %get-tuple-element.182) | copy-start | bytes 292
  144.4 10.5 %collective-permute-start.8 = (bf16[2,4,4,384]{3,2,1,0:T(4,128)(2,1)S(1)}, bf16[2,4,4,384]{3,2,1,0:T(4,128)(2,1)S(1)}, u32[]{:S(2)}, u32[]{:S(2)}) collective-permute-start(bf16[2,4,4,384]{3,2,1,0:T(4,128)(2,1)S(1)} %get-tuple-element.137), channel_id=1, source_target_pairs={{0,6},{1,7},{8,14},{9,15},{16,22},{17,23},{24,30},{25,31}} | collective-permute-start | bytes 73736 | tf_op jit(solution)/shard_map/ppermute | solution.py:13
  145.7 10.5 %collective-permute-start.15 = (bf16[2,4,4,384]{3,2,1,0:T(4,128)(2,1)S(1)}, bf16[2,4,4,384]{3,2,1,0:T(4,128)(2,1)S(1)}, u32[]{:S(2)}, u32[]{:S(2)}) collective-permute-start(bf16[2,4,4,384]{3,2,1,0:T(4,128)(2,1)S(1)} %get-tuple-element.138), channel_id=1, source_target_pairs={{6,0},{7,1},{14,8},{15,9},{22,16},{23,17},{30,24},{31,25}} | collective-permute-start | bytes 73736 | tf_op jit(solution)/shard_map/ppermute | solution.py:13
  147.0 16.1 %collective-permute-start.13 = (bf16[2,4,4,384]{3,2,1,0:T(4,128)(2,1)S(1)}, bf16[2,4,4,384]{3,2,1,0:T(4,128)(2,1)S(1)}, u32[]{:S(2)}, u32[]{:S(2)}) collective-permute-start(bf16[2,4,4,384]{3,2,1,0:T(4,128)(2,1)S(1)} %get-tuple-element.139), channel_id=1, source_target_pairs={{2,0},{4,2},{6,4},{3,1},{5,3},{7,5},{10,8},{12,10},{14,12},{11,9},... | collective-permute-start | bytes 73736 | tf_op jit(solution)/shard_map/ppermute | solution.py:13
  148.4 16.1 %collective-permute-start.10 = (bf16[2,4,4,384]{3,2,1,0:T(4,128)(2,1)S(1)}, bf16[2,4,4,384]{3,2,1,0:T(4,128)(2,1)S(1)}, u32[]{:S(2)}, u32[]{:S(2)}) collective-permute-start(bf16[2,4,4,384]{3,2,1,0:T(4,128)(2,1)S(1)} %get-tuple-element.140), channel_id=1, source_target_pairs={{0,2},{2,4},{4,6},{1,3},{3,5},{5,7},{8,10},{10,12},{12,14},{9,11},... | collective-permute-start | bytes 73736 | tf_op jit(solution)/shard_map/ppermute | solution.py:13
  152.9 11.6 %collective-permute-start.11 = (bf16[2,16,4,384]{3,2,1,0:T(4,128)(2,1)S(1)}, bf16[2,16,4,384]{3,2,1,0:T(4,128)(2,1)S(1)}, u32[]{:S(2)}, u32[]{:S(2)}) collective-permute-start(bf16[2,16,4,384]{3,2,1,0:T(4,128)(2,1)S(1)} %get-tuple-element.143), channel_id=1, source_target_pairs={{0,2},{2,4},{4,6},{1,3},{3,5},{5,7},{8,10},{10,12},{12,14},{9,11},... | collective-permute-start | bytes 294920 | tf_op jit(solution)/shard_map/ppermute | solution.py:13
  154.9 9.6 %collective-permute-start.12 = (bf16[2,16,4,384]{3,2,1,0:T(4,128)(2,1)S(1)}, bf16[2,16,4,384]{3,2,1,0:T(4,128)(2,1)S(1)}, u32[]{:S(2)}, u32[]{:S(2)}) collective-permute-start(bf16[2,16,4,384]{3,2,1,0:T(4,128)(2,1)S(1)} %get-tuple-element.144), channel_id=1, source_target_pairs={{2,0},{4,2},{6,4},{3,1},{5,3},{7,5},{10,8},{12,10},{14,12},{11,9},... | collective-permute-start | bytes 294920 | tf_op jit(solution)/shard_map/ppermute | solution.py:13
  156.2 9.6 %collective-permute-start.9 = (bf16[2,4,24,384]{3,2,1,0:T(8,128)(2,1)S(1)}, bf16[2,4,24,384]{3,2,1,0:T(8,128)(2,1)S(1)}, u32[]{:S(2)}, u32[]{:S(2)}) collective-permute-start(bf16[2,4,24,384]{3,2,1,0:T(8,128)(2,1)S(1)} %get-tuple-element.141), channel_id=1, source_target_pairs={{0,4},{2,6},{1,5},{3,7},{8,12},{10,14},{9,13},{11,15},{16,20},{18,... | collective-permute-start | bytes 442376 | tf_op jit(solution)/shard_map/ppermute | solution.py:13
  163.1 10.0 %collective-permute-start.14 = (bf16[2,4,24,384]{3,2,1,0:T(8,128)(2,1)S(1)}, bf16[2,4,24,384]{3,2,1,0:T(8,128)(2,1)S(1)}, u32[]{:S(2)}, u32[]{:S(2)}) collective-permute-start(bf16[2,4,24,384]{3,2,1,0:T(8,128)(2,1)S(1)} %get-tuple-element.142), channel_id=1, source_target_pairs={{4,0},{6,2},{5,1},{7,3},{12,8},{14,10},{13,9},{15,11},{20,16},{22,... | collective-permute-start | bytes 442376 | tf_op jit(solution)/shard_map/ppermute | solution.py:13
  (10 other events, 18.4 us)
Sparse Core Ops, SparseCore 0:
  9.2 40.0 all-gather.1
where the time goes:
time: 183 us; the launch traced here: 182 us
  starting transfers between devices  41.4 us (23%)
  waiting for transfers between devices  38.2 us (21%)
  local copies, waits for them, and re-layouts  31.3 us (17%)
  other arithmetic  26.4 us (14%)
  matrix products  22.5 us (12%)
  between operations  22.2 us (12%)
    ppermute x16, starting transfers between devices, passed_along(): return lax.ppermute(shard, axis, pairs)  41.4 us
    dot_general x9, matrix products, convolve(): jnp.dot(flattened, kernel[tap_time, tap_row].reshape(3 * channels, -1), p...  22.5 us
    all_gather x1, waiting for transfers between devices, local(): pieces = lax.all_gather(own_block[None], 'group', axis=0, tiled=True)  20.4 us
    ppermute x16, waiting for transfers between devices, passed_along(): return lax.ppermute(shard, axis, pairs)  17.1 us
    slice x2, local copies, waits for them, and re-layouts, convolve(): window[:, :, tap_col:tap_col + col_count]  10.8 us
    scatter x8, local copies, waits for them, and re-layouts, gather_rims(): result.at[:, row_dest:row_dest + row_len, col_dest:col_dest + col_len]  8.67 us
    another operation x6, other arithmetic  8.1 us
    concatenate x5, other arithmetic, convolve(): jnp.concatenate([window[:, :, tap_col:tap_col + col_count] for tap_col in...  8 us
  transfers between devices with their start and end apart: 17, of which 4 were waited for; matrix products, arithmetic and copies ran while one was open for 16% of the time, Pallas kernels for 0%

commit v1 on v0

--- a/solution.py
+++ b/solution.py
@@ -121,7 +121,14 @@
     reaches = margins[0]
     wanted = group_slot[lax.axis_index("group")] - 1
     chosen = jnp.zeros((2, core_h, core_w, channels), jnp.bfloat16)
-    pieces = lax.all_gather(own_block[None], "group", axis=0, tiled=True)
+    ring = [own_block[None]]
+    for hop in range(3):
+        ring.append(lax.ppermute(ring[-1], "group", [(dev, (dev + 1) % 4) for dev in range(4)]))
+    pieces = jnp.roll(
+        jnp.concatenate(ring[::-1], axis=0),
+        (lax.axis_index("group") + 1) * ring[0].shape[0],
+        axis=0,
+    )
     first_dev = jnp.int32(0)
     for offset in range(pieces.shape[0]):
         matches = group_slot[first_dev + offset] == wanted

time: 183 us -> 171 us (0.934)
  between operations: 22.2 us -> 8.68 us
  starting transfers between devices: 41.4 us -> 43.6 us
    ppermute x0 -> x3, waiting for transfers between devices: none -> 22.1 us  [local(): lax.ppermute(ring[-1], 'group', [(dev, (dev + 1) % 4) for dev in range(4)])]
    all_gather x1 -> x0, waiting for transfers between devices: 20.4 us -> none  [local(): pieces = lax.all_gather(own_block[None], 'group', axis=0, tiled=True)]
    ppermute x0 -> x3, starting transfers between devices: none -> 3.76 us  [local(): lax.ppermute(ring[-1], 'group', [(dev, (dev + 1) % 4) for dev in range(4)])]
  transfers between devices with their start and end apart: 17 -> 19, of which waited for: 4 -> 6; matrix products, arithmetic and copies ran while one was open for 16% -> 17% of each run, Pallas kernels for 0% -> 0%
where the time goes in v1:
time: 171 us; the launch traced here: 170 us
  starting transfers between devices  43.6 us (25%)
  waiting for transfers between devices  38.3 us (22%)
  local copies, waits for them, and re-layouts  32.3 us (19%)
  other arithmetic  25 us (15%)
  matrix products  22.5 us (13%)
  between operations  8.68 us (5%)
    ppermute x16, starting transfers between devices, passed_along(): return lax.ppermute(shard, axis, pairs)  39.9 us
    dot_general x9, matrix products, convolve(): jnp.dot(flattened, kernel[tap_time, tap_row].reshape(3 * channels, -1), p...  22.5 us
    ppermute x3, waiting for transfers between devices, local(): lax.ppermute(ring[-1], 'group', [(dev, (dev + 1) % 4) for dev in range(4)])  22.1 us
    ppermute x16, waiting for transfers between devices, passed_along(): return lax.ppermute(shard, axis, pairs)  16.1 us
    slice x2, local copies, waits for them, and re-layouts, convolve(): window[:, :, tap_col:tap_col + col_count]  10.8 us
    scatter x8, local copies, waits for them, and re-layouts, gather_rims(): result.at[:, row_dest:row_dest + row_len, col_dest:col_dest + col_len]  8.79 us
    another operation x6, other arithmetic  8.25 us
    concatenate x5, other arithmetic, convolve(): jnp.concatenate([window[:, :, tap_col:tap_col + col_count] for tap_col in...  8 us
  transfers between devices with their start and end apart: 19, of which 6 were waited for; matrix products, arithmetic and copies ran while one was open for 17% of the time, Pallas kernels for 0%

profile of v1, /device:TPU:0, one launch (start us, length us, event | category | flops | bytes accessed | tf_op | source)
XLA Modules:
  0.0 170.3 jit_solution(1979241398384574442)
XLA Ops:
  0.0 3.0 %collective-permute-start = (bf16[1,2,16,24,384]{4,3,2,1,0:T(8,128)(2,1)}, bf16[1,2,16,24,384]{4,3,2,1,0:T(8,128)(2,1)S(1)}, u32[]{:S(2)}, u32[]{:S(2)}) collective-permute-start(bf16[1,2,16,24,384]{4,3,2,1,0:T(8,128)(2,1)} %param.22), channel_id=1, source_target_pairs={{0,8},{8,16},{16,24},{24,0},{1,9},{9,17},{17,25},{25,1},{2,10},{10... | collective-permute-start | bytes 1769480 | tf_op jit(solution)/shard_map/ppermute | solution.py:126
  8.8 8.7 %collective-permute-done = bf16[1,2,16,24,384]{4,3,2,1,0:T(8,128)(2,1)S(1)} collective-permute-done((bf16[1,2,16,24,384]{4,3,2,1,0:T(8,128)(2,1)}, bf16[1,2,16,24,384]{4,3,2,1,0:T(8,128)(2,1)S(1)}, u32[]{:S(2)}, u32[]{:S(2)}) %collective-permute-start) | collective-permute-done | bytes 589856 | tf_op jit(solution)/shard_map/ppermute | solution.py:126
  23.1 9.7 %collective-permute-done.1 = bf16[1,2,16,24,384]{4,3,2,1,0:T(8,128)(2,1)S(1)} collective-permute-done((bf16[1,2,16,24,384]{4,3,2,1,0:T(8,128)(2,1)S(1)}, bf16[1,2,16,24,384]{4,3,2,1,0:T(8,128)(2,1)S(1)}, u32[]{:S(2)}, u32[]{:S(2)}) %collective-permute-start.1) | collective-permute-done | bytes 589856 | tf_op jit(solution)/shard_map/ppermute | solution.py:126
  37.9 5.7 %fusion.21 = (bf16[1,1,3,384,384]{4,3,2,1,0:T(8,128)(2,1)}, bf16[1,1,3,384,384]{4,3,2,1,0:T(8,128)(2,1)}, bf16[1,1,3,384,384]{4,3,2,1,0:T(8,128)(2,1)}, bf16[1,1...) fusion(bf16[3,3,3,384,384]{4,3,2,1,0:T(8,128)(2,1)} %param.26), kind=kLoop, calls=%fused_computation.100 | loop fusion | bytes 15925248 | tf_op jit(solution)/shard_map/slice | solution.py:35
  43.6 3.8 %collective-permute-done.2 = bf16[1,2,16,24,384]{4,3,2,1,0:T(8,128)(2,1)S(1)} collective-permute-done((bf16[1,2,16,24,384]{4,3,2,1,0:T(8,128)(2,1)S(1)}, bf16[1,2,16,24,384]{4,3,2,1,0:T(8,128)(2,1)S(1)}, u32[]{:S(2)}, u32[]{:S(2)}) %collective-permute-start.2) | collective-permute-done | bytes 589856 | tf_op jit(solution)/shard_map/ppermute | solution.py:126
  48.6 4.1 %collective-permute-start.4 = (bf16[4,4,24,384]{3,2,1,0:T(8,128)(2,1)S(1)}, bf16[4,4,24,384]{3,2,1,0:T(8,128)(2,1)S(1)}, u32[]{:S(2)}, u32[]{:S(2)}) collective-permute-start(bf16[4,4,24,384]{3,2,1,0:T(8,128)(2,1)S(1)} %get-tuple-element.150), channel_id=1, source_target_pairs={{0,4},{2,6},{1,5},{3,7},{8,12},{10,14},{9,13},{11,15},{16,20},{18,... | collective-permute-start | bytes 884744 | tf_op jit(solution)/shard_map/ppermute | solution.py:13
  53.5 2.3 %collective-permute-start.3 = (bf16[4,4,4,384]{3,2,1,0:T(4,128)(2,1)S(1)}, bf16[4,4,4,384]{3,2,1,0:T(4,128)(2,1)S(1)}, u32[]{:S(2)}, u32[]{:S(2)}) collective-permute-start(bf16[4,4,4,384]{3,2,1,0:T(4,128)(2,1)S(1)} %get-tuple-element.146), channel_id=1, source_target_pairs={{0,6},{1,7},{8,14},{9,15},{16,22},{17,23},{24,30},{25,31}} | collective-permute-start | bytes 147464 | tf_op jit(solution)/shard_map/ppermute | solution.py:13
  57.3 2.4 %collective-permute-start.5 = (bf16[4,4,4,384]{3,2,1,0:T(4,128)(2,1)}, bf16[4,4,4,384]{3,2,1,0:T(4,128)(2,1)}, u32[]{:S(2)}, u32[]{:S(2)}) collective-permute-start(bf16[4,4,4,384]{3,2,1,0:T(4,128)(2,1)} %get-tuple-element.147), channel_id=1, source_target_pairs={{0,2},{2,4},{4,6},{1,3},{3,5},{5,7},{8,10},{10,12},{12,14},{9,11},... | collective-permute-start | bytes 147464 | tf_op jit(solution)/shard_map/ppermute | solution.py:13
  63.2 5.9 %collective-permute-start.6 = (bf16[4,16,4,384]{3,2,1,0:T(4,128)(2,1)S(1)}, bf16[4,16,4,384]{3,2,1,0:T(4,128)(2,1)}, u32[]{:S(2)}, u32[]{:S(2)}) collective-permute-start(bf16[4,16,4,384]{3,2,1,0:T(4,128)(2,1)S(1)} %get-tuple-element.152), channel_id=1, source_target_pairs={{0,2},{2,4},{4,6},{1,3},{3,5},{5,7},{8,10},{10,12},{12,14},{9,11},... | collective-permute-start | bytes 589832 | tf_op jit(solution)/shard_map/ppermute | solution.py:13
  71.2 2.5 %scatter.29 = bf16[4,24,32,384]{3,2,1,0:T(8,128)(2,1)S(1)} dynamic-update-slice(bf16[4,24,32,384]{3,2,1,0:T(8,128)(2,1)S(1)} %constant_dynamic-update-slice_fusion.12, bf16[4,4,24,384]{3,2,1,0:T(8,128)(2,1)S(1)} %dynamic-slice_select_fusion.4, s32[]{:T(128)} %constant.294.clone.1, s32[]{:T(128)} %bitcast.10, s32[]{:T(128)} %bitcast.11, s32[]{:T(128)} %constant.294.clone.1) | dynamic-update-slice | bytes 589828 | tf_op jit(solution)/shard_map/scatter | solution.py:111
  75.2 3.3 %dynamic-slice_select_fusion.5 = bf16[4,4,4,384]{3,2,1,0:T(4,128)(2,1)} fusion(bf16[4,4,4,384]{3,2,1,0:T(4,128)(2,1)} %collective-permute-done.5, bf16[4,24,32,384]{3,2,1,0:T(8,128)(2,1)S(1)} %scatter.29, s32[]{:T(128)} %bitcast.12, s32[]{:T(128)} %bitcast.13, pred[]{:T(512)} %and_reduce_fusion), kind=kLoop, calls=%fused_computation.66 | loop fusion | flops 24576 | bytes 147465 | tf_op jit(solution)/shard_map/select.10
  78.5 2.2 %scatter.30 = bf16[4,24,32,384]{3,2,1,0:T(8,128)(2,1)S(1)} dynamic-update-slice(bf16[4,24,32,384]{3,2,1,0:T(8,128)(2,1)S(1)} %scatter.29, bf16[4,4,4,384]{3,2,1,0:T(4,128)(2,1)} %dynamic-slice_select_fusion.5, s32[]{:T(128)} %constant.294.clone.1, s32[]{:T(128)} %bitcast.12, s32[]{:T(128)} %bitcast.13, s32[]{:T(128)} %constant.294.clone.1) | dynamic-update-slice | bytes 98308 | tf_op jit(solution)/shard_map/scatter | solution.py:111
  82.7 7.5 %collective-permute-done.9 = bf16[4,4,24,384]{3,2,1,0:T(8,128)(2,1)S(1)} collective-permute-done((bf16[4,4,24,384]{3,2,1,0:T(8,128)(2,1)S(1)}, bf16[4,4,24,384]{3,2,1,0:T(8,128)(2,1)S(1)}, u32[]{:S(2)}, u32[]{:S(2)}) %collective-permute-start.9) | collective-permute-done | bytes 294944 | tf_op jit(solution)/shard_map/ppermute | solution.py:13
  92.9 2.2 %fusion.7 = bf16[4,24,32,384]{3,2,1,0:T(8,128)(2,1)S(1)} fusion(bf16[4,24,32,384]{3,2,1,0:T(8,128)(2,1)S(1)} %constant_dynamic-update-slice_fusion.8, f32[384]{0:T(512)} %param.25, f32[4,24,32]{2,1,0:T(8,128)S(1)} %add_rsqrt_fusion), kind=kLoop, calls=%fused_computation.9 | loop fusion | flops 9437184 | bytes 4732416 | tf_op jit(solution)/shard_map/convert_element_type | solution.py:19
  96.6 4.5 %fusion.23 = (bf16[2,24,32,384]{3,2,1,0:T(8,128)(2,1)S(1)}, bf16[2,24,32,384]{3,2,1,0:T(8,128)(2,1)S(1)}, bf16[2,24,32,384]{3,2,1,0:T(8,128)(2,1)}, bf16[2,24,32...) fusion(bf16[4,26,34,384]{3,2,1,0:T(8,128)(2,1)S(1)} %pad_select, ...), kind=kLoop, calls=%fused_computation.102 | loop fusion | bytes 18874368 | tf_op jit(solution)/shard_map/slice | solution.py:30
  101.1 6.3 %fusion.22 = (bf16[2,24,32,384]{3,2,1,0:T(8,128)(2,1)}, bf16[2,24,32,384]{3,2,1,0:T(8,128)(2,1)}, bf16[2,24,32,384]{3,2,1,0:T(8,128)(2,1)}, bf16[2,24,32,384]{3,...) fusion(bf16[4,26,34,384]{3,2,1,0:T(8,128)(2,1)S(1)} %pad_select, ...), kind=kLoop, calls=%fused_computation.101 | loop fusion | bytes 44826624 | tf_op jit(solution)/shard_map/slice | solution.py:30
  107.4 3.4 %pad_maximum_fusion = (bf16[2,24,32,1152]{3,2,1,0:T(8,128)(2,1)S(1)}, bf16[2,24,32,1152]{3,2,1,0:T(8,128)(2,1)S(1)}) fusion(bf16[2,24,32,384]{3,2,1,0:T(8,128)(2,1)} %get-tuple-element.134, bf16[2,24,32,384]{3,2,1,0:T(8,128)(2,1)} %get-tuple-element.135, bf16[2,24,32,384]{3,2,1,0:T(8,128)(2,1)} %get-tuple-element.136, ...), kind=kLoop, calls=%fused_computation.10 | loop fusion | flops 21233664 | bytes 14155776 | tf_op jit(solution)/shard_map/concatenate | solution.py:29
  113.0 3.6 %convolution_add_fusion.7 = f32[1536,384]{1,0:T(8,128)} fusion(f32[1536,384]{1,0:T(8,128)S(1)} %fusion.31, bf16[1536,1152]{1,0:T(8,128)(2,1)S(1)} %bitcast.65, bf16[1152,384]{1,0:T(8,128)(2,1)S(1)} %bitcast.79), kind=kOutput, calls=%fused_computation.27 | convolution fusion | flops 1359544320 | bytes 9142272 | tf_op jit(solution)/shard_map/dot_general | solution.py:33
  119.7 3.9 %convolution_add_fusion.6 = f32[1536,384]{1,0:T(8,128)S(1)} fusion(f32[1536,384]{1,0:T(8,128)} %convolution_add_fusion.7, bf16[1536,1152]{1,0:T(8,128)(2,1)S(1)} %bitcast.66, bf16[1152,384]{1,0:T(8,128)(2,1)S(1)} %bitcast.78), kind=kOutput, calls=%fused_computation.26 | convolution fusion | flops 1359544320 | bytes 9142272 | tf_op jit(solution)/shard_map/dot_general | solution.py:33
  127.0 2.2 %convolution_add_fusion.4 = f32[1536,384]{1,0:T(8,128)S(1)} fusion(f32[1536,384]{1,0:T(8,128)S(1)} %convolution_add_fusion.5, bf16[1536,1152]{1,0:T(8,128)(2,1)S(1)} %bitcast.67, bf16[1152,384]{1,0:T(8,128)(2,1)S(1)} %bitcast.76), kind=kOutput, calls=%fused_computation.24 | convolution fusion | flops 1359544320 | bytes 9142272 | tf_op jit(solution)/shard_map/dot_general | solution.py:33
  132.5 2.2 %convolution_add_fusion.2 = f32[1536,384]{1,0:T(8,128)S(1)} fusion(f32[1536,384]{1,0:T(8,128)S(1)} %convolution_add_fusion.3, bf16[1536,1152]{1,0:T(8,128)(2,1)S(1)} %bitcast.68, bf16[1152,384]{1,0:T(8,128)(2,1)S(1)} %bitcast.74), kind=kOutput, calls=%fused_computation.22 | convolution fusion | flops 1359544320 | bytes 9142272 | tf_op jit(solution)/shard_map/dot_general | solution.py:33
  143.5 4.5 %collective-permute-start.13 = (bf16[2,4,4,384]{3,2,1,0:T(4,128)(2,1)S(1)}, bf16[2,4,4,384]{3,2,1,0:T(4,128)(2,1)S(1)}, u32[]{:S(2)}, u32[]{:S(2)}) collective-permute-start(bf16[2,4,4,384]{3,2,1,0:T(4,128)(2,1)S(1)} %get-tuple-element.140), channel_id=1, source_target_pairs={{0,2},{2,4},{4,6},{1,3},{3,5},{5,7},{8,10},{10,12},{12,14},{9,11},... | collective-permute-start | bytes 73736 | tf_op jit(solution)/shard_map/ppermute | solution.py:13
  151.3 6.9 %collective-permute-start.12 = (bf16[2,4,24,384]{3,2,1,0:T(8,128)(2,1)S(1)}, bf16[2,4,24,384]{3,2,1,0:T(8,128)(2,1)S(1)}, u32[]{:S(2)}, u32[]{:S(2)}) collective-permute-start(bf16[2,4,24,384]{3,2,1,0:T(8,128)(2,1)S(1)} %get-tuple-element.141), channel_id=1, source_target_pairs={{0,4},{2,6},{1,5},{3,7},{8,12},{10,14},{9,13},{11,15},{16,20},{18,... | collective-permute-start | bytes 442376 | tf_op jit(solution)/shard_map/ppermute | solution.py:13
  160.9 7.3 %collective-permute-done.17 = bf16[2,4,24,384]{3,2,1,0:T(8,128)(2,1)S(1)} collective-permute-done((bf16[2,4,24,384]{3,2,1,0:T(8,128)(2,1)S(1)}, bf16[2,4,24,384]{3,2,1,0:T(8,128)(2,1)S(1)}, u32[]{:S(2)}, u32[]{:S(2)}) %collective-permute-start.17) | collective-permute-done | bytes 147488 | tf_op jit(solution)/shard_map/ppermute | solution.py:13
  (113 shorter events, 53.6 us)
Async XLA Ops:
  0.0 17.5 %collective-permute-start = (bf16[1,2,16,24,384]{4,3,2,1,0:T(8,128)(2,1)}, bf16[1,2,16,24,384]{4,3,2,1,0:T(8,128)(2,1)S(1)}, u32[]{:S(2)}, u32[]{:S(2)}) collective-permute-start(bf16[1,2,16,24,384]{4,3,2,1,0:T(8,128)(2,1)} %param.22), channel_id=1, source_target_pairs={{0,8},{8,16},{16,24},{24,0},{1,9},{9,17},{17,25},{25,1},{2,10},{10... | collective-permute-start | bytes 1769480 | tf_op jit(solution)/shard_map/ppermute | solution.py:126
  17.5 15.4 %collective-permute-start.1 = (bf16[1,2,16,24,384]{4,3,2,1,0:T(8,128)(2,1)S(1)}, bf16[1,2,16,24,384]{4,3,2,1,0:T(8,128)(2,1)S(1)}, u32[]{:S(2)}, u32[]{:S(2)}) collective-permute-start(bf16[1,2,16,24,384]{4,3,2,1,0:T(8,128)(2,1)S(1)} %collective-permute-done), channel_id=1, source_target_pairs={{0,8},{8,16},{16,24},{24,0},{1,9},{9,17},{17,25},{25,1},{2,10},{10... | collective-permute-start | bytes 1769480 | tf_op jit(solution)/shard_map/ppermute | solution.py:126
  32.9 14.5 %collective-permute-start.2 = (bf16[1,2,16,24,384]{4,3,2,1,0:T(8,128)(2,1)S(1)}, bf16[1,2,16,24,384]{4,3,2,1,0:T(8,128)(2,1)S(1)}, u32[]{:S(2)}, u32[]{:S(2)}) collective-permute-start(bf16[1,2,16,24,384]{4,3,2,1,0:T(8,128)(2,1)S(1)} %collective-permute-done.1), channel_id=1, source_target_pairs={{0,8},{8,16},{16,24},{24,0},{1,9},{9,17},{17,25},{25,1},{2,10},{10... | collective-permute-start | bytes 1769480 | tf_op jit(solution)/shard_map/ppermute | solution.py:126
  43.6 4.0 %copy-start = (bf16[1,2,16,24,384]{4,3,2,1,0:T(8,128)(2,1)S(1)}, bf16[1,2,16,24,384]{4,3,2,1,0:T(8,128)(2,1)}, u32[]{:S(2)}) copy-start(bf16[1,2,16,24,384]{4,3,2,1,0:T(8,128)(2,1)} %param.22) | copy-start | bytes 1769476
  48.6 14.6 %collective-permute-start.4 = (bf16[4,4,24,384]{3,2,1,0:T(8,128)(2,1)S(1)}, bf16[4,4,24,384]{3,2,1,0:T(8,128)(2,1)S(1)}, u32[]{:S(2)}, u32[]{:S(2)}) collective-permute-start(bf16[4,4,24,384]{3,2,1,0:T(8,128)(2,1)S(1)} %get-tuple-element.150), channel_id=1, source_target_pairs={{0,4},{2,6},{1,5},{3,7},{8,12},{10,14},{9,13},{11,15},{16,20},{18,... | collective-permute-start | bytes 884744 | tf_op jit(solution)/shard_map/ppermute | solution.py:13
  53.5 8.4 %collective-permute-start.3 = (bf16[4,4,4,384]{3,2,1,0:T(4,128)(2,1)S(1)}, bf16[4,4,4,384]{3,2,1,0:T(4,128)(2,1)S(1)}, u32[]{:S(2)}, u32[]{:S(2)}) collective-permute-start(bf16[4,4,4,384]{3,2,1,0:T(4,128)(2,1)S(1)} %get-tuple-element.146), channel_id=1, source_target_pairs={{0,6},{1,7},{8,14},{9,15},{16,22},{17,23},{24,30},{25,31}} | collective-permute-start | bytes 147464 | tf_op jit(solution)/shard_map/ppermute | solution.py:13
  56.0 35.4 %collective-permute-start.10 = (bf16[4,4,4,384]{3,2,1,0:T(4,128)(2,1)}, bf16[4,4,4,384]{3,2,1,0:T(4,128)(2,1)}, u32[]{:S(2)}, u32[]{:S(2)}) collective-permute-start(bf16[4,4,4,384]{3,2,1,0:T(4,128)(2,1)} %get-tuple-element.145), channel_id=1, source_target_pairs={{6,0},{7,1},{14,8},{15,9},{22,16},{23,17},{30,24},{31,25}} | collective-permute-start | bytes 147464 | tf_op jit(solution)/shard_map/ppermute | solution.py:13
  57.3 16.4 %collective-permute-start.5 = (bf16[4,4,4,384]{3,2,1,0:T(4,128)(2,1)}, bf16[4,4,4,384]{3,2,1,0:T(4,128)(2,1)}, u32[]{:S(2)}, u32[]{:S(2)}) collective-permute-start(bf16[4,4,4,384]{3,2,1,0:T(4,128)(2,1)} %get-tuple-element.147), channel_id=1, source_target_pairs={{0,2},{2,4},{4,6},{1,3},{3,5},{5,7},{8,10},{10,12},{12,14},{9,11},... | collective-permute-start | bytes 147464 | tf_op jit(solution)/shard_map/ppermute | solution.py:13
  59.8 22.1 %collective-permute-start.8 = (bf16[4,4,4,384]{3,2,1,0:T(4,128)(2,1)}, bf16[4,4,4,384]{3,2,1,0:T(4,128)(2,1)}, u32[]{:S(2)}, u32[]{:S(2)}) collective-permute-start(bf16[4,4,4,384]{3,2,1,0:T(4,128)(2,1)} %get-tuple-element.148), channel_id=1, source_target_pairs={{2,0},{4,2},{6,4},{3,1},{5,3},{7,5},{10,8},{12,10},{14,12},{11,9},... | collective-permute-start | bytes 147464 | tf_op jit(solution)/shard_map/ppermute | solution.py:13
  61.9 19.9 %collective-permute-start.7 = (bf16[4,16,4,384]{3,2,1,0:T(4,128)(2,1)S(1)}, bf16[4,16,4,384]{3,2,1,0:T(4,128)(2,1)S(1)}, u32[]{:S(2)}, u32[]{:S(2)}) collective-permute-start(bf16[4,16,4,384]{3,2,1,0:T(4,128)(2,1)S(1)} %get-tuple-element.151), channel_id=1, source_target_pairs={{2,0},{4,2},{6,4},{3,1},{5,3},{7,5},{10,8},{12,10},{14,12},{11,9},... | collective-permute-start | bytes 589832 | tf_op jit(solution)/shard_map/ppermute | solution.py:13
  63.2 17.4 %collective-permute-start.6 = (bf16[4,16,4,384]{3,2,1,0:T(4,128)(2,1)S(1)}, bf16[4,16,4,384]{3,2,1,0:T(4,128)(2,1)}, u32[]{:S(2)}, u32[]{:S(2)}) collective-permute-start(bf16[4,16,4,384]{3,2,1,0:T(4,128)(2,1)S(1)} %get-tuple-element.152), channel_id=1, source_target_pairs={{0,2},{2,4},{4,6},{1,3},{3,5},{5,7},{8,10},{10,12},{12,14},{9,11},... | collective-permute-start | bytes 589832 | tf_op jit(solution)/shard_map/ppermute | solution.py:13
  73.7 16.6 %collective-permute-start.9 = (bf16[4,4,24,384]{3,2,1,0:T(8,128)(2,1)S(1)}, bf16[4,4,24,384]{3,2,1,0:T(8,128)(2,1)S(1)}, u32[]{:S(2)}, u32[]{:S(2)}) collective-permute-start(bf16[4,4,24,384]{3,2,1,0:T(8,128)(2,1)S(1)} %get-tuple-element.149), channel_id=1, source_target_pairs={{4,0},{6,2},{5,1},{7,3},{12,8},{14,10},{13,9},{15,11},{20,16},{22,... | collective-permute-start | bytes 884744 | tf_op jit(solution)/shard_map/ppermute | solution.py:13
  112.9 3.7 %copy-start.2 = (bf16[2,24,32,384]{3,2,1,0:T(8,128)(2,1)S(1)}, bf16[2,24,32,384]{3,2,1,0:T(8,128)(2,1)}, u32[]{:S(2)}) copy-start(bf16[2,24,32,384]{3,2,1,0:T(8,128)(2,1)} %get-tuple-element.110) | copy-start | bytes 3538948
  113.0 3.7 %copy-start.3 = (bf16[2,24,32,384]{3,2,1,0:T(8,128)(2,1)S(1)}, bf16[2,24,32,384]{3,2,1,0:T(8,128)(2,1)}, u32[]{:S(2)}) copy-start(bf16[2,24,32,384]{3,2,1,0:T(8,128)(2,1)} %get-tuple-element.111) | copy-start | bytes 3538948
  119.7 3.9 %copy-start.11 = (bf16[1,1,3,384,384]{4,3,2,1,0:T(8,128)(2,1)S(1)}, bf16[1,1,3,384,384]{4,3,2,1,0:T(8,128)(2,1)}, u32[]{:S(2)}) copy-start(bf16[1,1,3,384,384]{4,3,2,1,0:T(8,128)(2,1)} %get-tuple-element.105) | copy-start | bytes 2654212
  139.1 20.5 %copy-start.15 = (f32[24]{0:T(128)S(1)}, f32[24]{0:T(128)}, u32[]{:S(2)}) copy-start(f32[24]{0:T(128)} %get-tuple-element.182) | copy-start | bytes 292
  139.5 10.5 %collective-permute-start.11 = (bf16[2,4,4,384]{3,2,1,0:T(4,128)(2,1)S(1)}, bf16[2,4,4,384]{3,2,1,0:T(4,128)(2,1)S(1)}, u32[]{:S(2)}, u32[]{:S(2)}) collective-permute-start(bf16[2,4,4,384]{3,2,1,0:T(4,128)(2,1)S(1)} %get-tuple-element.137), channel_id=1, source_target_pairs={{0,6},{1,7},{8,14},{9,15},{16,22},{17,23},{24,30},{25,31}} | collective-permute-start | bytes 73736 | tf_op jit(solution)/shard_map/ppermute | solution.py:13
  140.8 10.5 %collective-permute-start.18 = (bf16[2,4,4,384]{3,2,1,0:T(4,128)(2,1)S(1)}, bf16[2,4,4,384]{3,2,1,0:T(4,128)(2,1)S(1)}, u32[]{:S(2)}, u32[]{:S(2)}) collective-permute-start(bf16[2,4,4,384]{3,2,1,0:T(4,128)(2,1)S(1)} %get-tuple-element.138), channel_id=1, source_target_pairs={{6,0},{7,1},{14,8},{15,9},{22,16},{23,17},{30,24},{31,25}} | collective-permute-start | bytes 73736 | tf_op jit(solution)/shard_map/ppermute | solution.py:13
  142.1 16.1 %collective-permute-start.16 = (bf16[2,4,4,384]{3,2,1,0:T(4,128)(2,1)S(1)}, bf16[2,4,4,384]{3,2,1,0:T(4,128)(2,1)S(1)}, u32[]{:S(2)}, u32[]{:S(2)}) collective-permute-start(bf16[2,4,4,384]{3,2,1,0:T(4,128)(2,1)S(1)} %get-tuple-element.139), channel_id=1, source_target_pairs={{2,0},{4,2},{6,4},{3,1},{5,3},{7,5},{10,8},{12,10},{14,12},{11,9},... | collective-permute-start | bytes 73736 | tf_op jit(solution)/shard_map/ppermute | solution.py:13
  143.5 16.1 %collective-permute-start.13 = (bf16[2,4,4,384]{3,2,1,0:T(4,128)(2,1)S(1)}, bf16[2,4,4,384]{3,2,1,0:T(4,128)(2,1)S(1)}, u32[]{:S(2)}, u32[]{:S(2)}) collective-permute-start(bf16[2,4,4,384]{3,2,1,0:T(4,128)(2,1)S(1)} %get-tuple-element.140), channel_id=1, source_target_pairs={{0,2},{2,4},{4,6},{1,3},{3,5},{5,7},{8,10},{10,12},{12,14},{9,11},... | collective-permute-start | bytes 73736 | tf_op jit(solution)/shard_map/ppermute | solution.py:13
  148.1 11.6 %collective-permute-start.14 = (bf16[2,16,4,384]{3,2,1,0:T(4,128)(2,1)S(1)}, bf16[2,16,4,384]{3,2,1,0:T(4,128)(2,1)S(1)}, u32[]{:S(2)}, u32[]{:S(2)}) collective-permute-start(bf16[2,16,4,384]{3,2,1,0:T(4,128)(2,1)S(1)} %get-tuple-element.143), channel_id=1, source_target_pairs={{0,2},{2,4},{4,6},{1,3},{3,5},{5,7},{8,10},{10,12},{12,14},{9,11},... | collective-permute-start | bytes 294920 | tf_op jit(solution)/shard_map/ppermute | solution.py:13
  150.0 9.6 %collective-permute-start.15 = (bf16[2,16,4,384]{3,2,1,0:T(4,128)(2,1)S(1)}, bf16[2,16,4,384]{3,2,1,0:T(4,128)(2,1)S(1)}, u32[]{:S(2)}, u32[]{:S(2)}) collective-permute-start(bf16[2,16,4,384]{3,2,1,0:T(4,128)(2,1)S(1)} %get-tuple-element.144), channel_id=1, source_target_pairs={{2,0},{4,2},{6,4},{3,1},{5,3},{7,5},{10,8},{12,10},{14,12},{11,9},... | collective-permute-start | bytes 294920 | tf_op jit(solution)/shard_map/ppermute | solution.py:13
  151.3 9.6 %collective-permute-start.12 = (bf16[2,4,24,384]{3,2,1,0:T(8,128)(2,1)S(1)}, bf16[2,4,24,384]{3,2,1,0:T(8,128)(2,1)S(1)}, u32[]{:S(2)}, u32[]{:S(2)}) collective-permute-start(bf16[2,4,24,384]{3,2,1,0:T(8,128)(2,1)S(1)} %get-tuple-element.141), channel_id=1, source_target_pairs={{0,4},{2,6},{1,5},{3,7},{8,12},{10,14},{9,13},{11,15},{16,20},{18,... | collective-permute-start | bytes 442376 | tf_op jit(solution)/shard_map/ppermute | solution.py:13
  158.2 10.0 %collective-permute-start.17 = (bf16[2,4,24,384]{3,2,1,0:T(8,128)(2,1)S(1)}, bf16[2,4,24,384]{3,2,1,0:T(8,128)(2,1)S(1)}, u32[]{:S(2)}, u32[]{:S(2)}) collective-permute-start(bf16[2,4,24,384]{3,2,1,0:T(8,128)(2,1)S(1)} %get-tuple-element.142), channel_id=1, source_target_pairs={{4,0},{6,2},{5,1},{7,3},{12,8},{14,10},{13,9},{15,11},{20,16},{22,... | collective-permute-start | bytes 442376 | tf_op jit(solution)/shard_map/ppermute | solution.py:13
  (12 other events, 25.5 us)
